TPU v7x, 128 devices: a whole 4x4x4 slice. The times are simulated.
128 devices in a mesh: fsdp: 64 (over z, y, x), tensor: 2 (over core).
Axes of the slice: x: 4, y: 4, z: 4, core: 2. Of those that a mesh axis runs over, the one named last changes fastest.
Arguments:
- weights: bfloat16 [64, 1792, 256], P(None, 'fsdp', 'tensor'), may hold values from -0.125 to 0.125
- gradient: bfloat16 [64, 1792, 256], P(None, 'fsdp', 'tensor'), may hold values from -6 to 6
- moment_first: float32 [64, 1792, 256], P('fsdp', None, 'tensor'), may hold values from -4 to 4
- moment_second: float32 [64, 1792, 256], P('fsdp', None, 'tensor'), may hold values from 0.05 to 4
- statistics: float32 [64, 8, 256, 256], P('fsdp', 'tensor'), may hold values from -0.4 to 4.4, as said below
- eigenbases: float32 [64, 8, 256, 256], P('fsdp', 'tensor'), may hold values from -0.2 to 1.2
Outputs:
- new_weights: bfloat16 [64, 1792, 256], P(None, 'fsdp', 'tensor')
- new_first: float32 [64, 1792, 256], P('fsdp', None, 'tensor')
- new_second: float32 [64, 1792, 256], P('fsdp', None, 'tensor')
- new_statistics: float32 [64, 8, 256, 256], P('fsdp', 'tensor')
- new_bases: float32 [64, 8, 256, 256], P('fsdp', 'tensor')
Inputs may be any that keep to these rules, and one draw needn't show every extreme that they name: `statistics`: symmetric matrices.
All inputs are finite; a program needn't handle non-finite values.
Results may differ from a plain program's by a relative error of at most 0.0095.
Values may be sent and summed in bfloat16 or wider, within the bound.
A program may use at most 64 MiB of HBM per device.

v0:
```python
import functools

import jax
import jax.numpy as jnp
from jax import lax
from jax.experimental import pallas as pl
from jax.experimental.pallas import tpu as pltpu
from jax.sharding import PartitionSpec as P

NS_STEPS = 5
STEP = 10
MESH = pl.DeviceIdType.MESH
LOW = jnp.bfloat16
NN = (((1,), (0,)), ((), ()))
NT = (((1,), (1,)), ((), ()))
TN = (((0,), (0,)), ((), ()))


def product(a, b, dims):
    return lax.dot_general(a, b, dims, preferred_element_type=jnp.float32)


def halves(x):
    high = x.astype(LOW)
    return high, (x - high.astype(jnp.float32)).astype(LOW)


def product3(a, b, dims):
    return (
        product(a[0], b[1], dims) + product(a[1], b[0], dims) + product(a[0], b[0], dims)
    )


def kernel(
    ndev,
    weights, gradient, moment_first, moment_second, statistics, eigenbases,
    new_weights, new_first, new_second, new_statistics, new_bases,
    grad_mine, grad_other, grad_wide, grad_full, bases_low, dir_mine, dir_other,
    update_wide, update_out, update_in,
    send_grad, recv_grad, send_update, recv_update,
    send_pair, recv_pair, send_dir, recv_dir, local_sem,
):
    me = lax.axis_index("fsdp")
    core = lax.axis_index("tensor")
    other = 1 - core
    part = gradient.shape[1]
    cols = gradient.shape[2]
    per = eigenbases.shape[0]
    block = eigenbases.shape[1]
    rows = moment_first.shape[0]
    nblk = rows // block
    my_cols = pl.ds(pl.multiple_of(core * cols, cols), cols)
    other_cols = pl.ds(pl.multiple_of(other * cols, cols), cols)

    for j in range(per):
        bases_low[core * per + j] = eigenbases[j].astype(LOW)

    barrier = pltpu.get_barrier_semaphore()

    def greet(i, carry):
        pl.semaphore_signal(
            barrier, inc=1, device_id=(lax.rem(me + i, ndev), core), device_id_type=MESH
        )
        return carry

    lax.fori_loop(1, ndev, greet, 0)
    pl.semaphore_signal(barrier, inc=1, device_id=(me, other), device_id_type=MESH)
    pl.semaphore_wait(barrier, ndev)

    def grad_copy(i):
        peer = lax.rem(me + i, ndev)
        return pltpu.make_async_remote_copy(
            src_ref=gradient.at[peer],
            dst_ref=grad_mine.at[me],
            send_sem=send_grad.at[i],
            recv_sem=recv_grad.at[i],
            device_id=(peer, core),
            device_id_type=MESH,
        )

    def update_copy(i):
        peer = lax.rem(me + i, ndev)
        return pltpu.make_async_remote_copy(
            src_ref=update_out.at[peer],
            dst_ref=update_in.at[me],
            send_sem=send_update.at[i],
            recv_sem=recv_update.at[i],
            device_id=(peer, core),
            device_id_type=MESH,
        )

    def grad_wait(i):
        source = lax.rem(me + ndev - i, ndev)
        return pltpu.make_async_remote_copy(
            src_ref=gradient.at[source],
            dst_ref=grad_mine.at[source],
            send_sem=send_grad.at[i],
            recv_sem=recv_grad.at[i],
            device_id=(source, core),
            device_id_type=MESH,
        )

    def update_wait(i):
        source = lax.rem(me + ndev - i, ndev)
        return pltpu.make_async_remote_copy(
            src_ref=update_out.at[source],
            dst_ref=update_in.at[source],
            send_sem=send_update.at[i],
            recv_sem=recv_update.at[i],
            device_id=(source, core),
            device_id_type=MESH,
        )

    def start(make):
        def step(i, carry):
            make(i).start()
            return carry

        lax.fori_loop(1, ndev, step, 0)

    def arrived(make):
        def step(i, carry):
            make(i).wait_recv()
            return carry

        lax.fori_loop(1, ndev, step, 0)

    def sent(make):
        def step(i, carry):
            make(i).wait_send()
            return carry

        lax.fori_loop(1, ndev, step, 0)

    start(grad_copy)
    own = pltpu.make_async_copy(gradient.at[me], grad_mine.at[me], local_sem.at[0])
    own.start()
    mine = bases_low.at[pl.ds(core * per, per)]
    share_bases = pltpu.make_async_remote_copy(
        src_ref=mine,
        dst_ref=mine,
        send_sem=send_pair.at[0],
        recv_sem=recv_pair.at[0],
        device_id=(me, other),
        device_id_type=MESH,
    )
    share_bases.start()
    own.wait()
    arrived(grad_wait)
    share_grad = pltpu.make_async_remote_copy(
        src_ref=grad_mine,
        dst_ref=grad_other,
        send_sem=send_pair.at[1],
        recv_sem=recv_pair.at[1],
        device_id=(me, other),
        device_id_type=MESH,
    )
    share_grad.start()

    for s in range(ndev):
        grad_wide[s * part : (s + 1) * part, :] = grad_mine[s].astype(jnp.float32)
    grad_full[:, my_cols] = grad_wide[...].astype(LOW)
    share_bases.wait()
    share_grad.wait()
    for s in range(ndev):
        grad_wide[s * part : (s + 1) * part, :] = grad_other[s].astype(jnp.float32)
    grad_full[:, other_cols] = grad_wide[...].astype(LOW)

    right_cols = bases_low[nblk, :, my_cols]

    def dir_copy(k):
        here = pl.ds(k * block, block)
        return pltpu.make_async_remote_copy(
            src_ref=dir_mine.at[here],
            dst_ref=dir_other.at[here],
            send_sem=send_dir.at[k],
            recv_sem=recv_dir.at[k],
            device_id=(me, other),
            device_id_type=MESH,
        )

    for k in range(nblk):
        here = slice(k * block, (k + 1) * block)
        half_turn = product(grad_full[here, :], right_cols, NN).astype(LOW)
        rotated = product(bases_low[k], half_turn, TN)
        first = 0.9 * moment_first[here, :] + 0.1 * rotated
        second = 0.95 * moment_second[here, :] + 0.05 * rotated * rotated
        new_first[here, :] = first
        new_second[here, :] = second
        dir_mine[here, :] = (
            first / (1.0 - 0.9**STEP) / (jnp.sqrt(second / (1.0 - 0.95**STEP)) + 1e-08)
        ).astype(LOW)
        if k >= 1:
            dir_copy(k - 1).start()

    def put_gram(j, gram):
        new_statistics[j] = 0.95 * statistics[j] + 0.05 * gram

    def left_gram(j):
        g = grad_full[pl.ds(pl.multiple_of((core * per + j) * block, block), block), :]
        put_gram(j, product(g, g, NT))

    left_gram(0)
    dir_copy(nblk - 1).start()
    for j in range(1, per - 1):
        left_gram(j)

    @pl.when(core == 0)
    def _():
        left_gram(per - 1)

    @pl.when(core == 1)
    def _():
        put_gram(per - 1, product(grad_full[...], grad_full[...], TN))

    right_rows = bases_low.at[nblk]
    rows_mine = right_rows[my_cols, my_cols]
    rows_other = right_rows[my_cols, other_cols]
    for k in range(nblk):
        here = slice(k * block, (k + 1) * block)
        dir_copy(k).wait()
        turned = product(dir_mine[here, :], rows_mine, NT)
        turned = (turned + product(dir_other[here, :], rows_other, NT)).astype(LOW)
        update = product(bases_low[k], turned, NN).astype(LOW)
        update_wide[here, :] = update.astype(jnp.float32)
    for s in range(ndev):
        update_out[s] = update_wide[s * part : (s + 1) * part, :].astype(LOW)

    growns = []
    for j in range(per):
        grown = product3(halves(new_statistics[j]), halves(eigenbases[j]), NN)
        growns.append(grown)
        new_bases[j] = grown / (jnp.sqrt(jnp.sum(grown * grown)) + 1e-06)

    start(update_copy)
    own = pltpu.make_async_copy(update_out.at[me], update_in.at[me], local_sem.at[1])
    own.start()

    def sweep(step, carry):
        for j in range(per):
            x = new_bases[j]
            parts = halves(x)
            outer = product3(parts, parts, NT)
            new_bases[j] = 1.5 * x - 0.5 * product3(halves(outer), parts, NN)
        return carry

    lax.fori_loop(0, NS_STEPS, sweep, 0)
    sent(grad_copy)
    own.wait()
    arrived(update_wait)

    def finish(s, carry):
        w = weights[s].astype(jnp.float32)
        u = update_in[s].astype(jnp.float32)
        new_weights[s] = (w - 0.01 * (u + 0.1 * w)).astype(LOW)
        return carry

    lax.fori_loop(0, ndev, finish, 0)
    sent(update_copy)


def body(ndev, weights, gradient, moment_first, moment_second, statistics, eigenbases):
    part, cols = gradient.shape[1:]
    rows = moment_first.shape[1]
    per, block = eigenbases.shape[1:3]
    nblk = rows // block
    vmem = pl.BlockSpec(memory_space=pltpu.VMEM)
    f32 = jnp.float32
    dma = pltpu.SemaphoreType.DMA
    inputs = (
        weights, gradient, moment_first[0], moment_second[0], statistics[0], eigenbases[0]
    )
    outs = pl.pallas_call(
        functools.partial(kernel, ndev),
        out_shape=(
            jax.ShapeDtypeStruct(weights.shape, LOW),
            jax.ShapeDtypeStruct((rows, cols), f32),
            jax.ShapeDtypeStruct((rows, cols), f32),
            jax.ShapeDtypeStruct((per, block, block), f32),
            jax.ShapeDtypeStruct((per, block, block), f32),
        ),
        in_specs=[vmem] * 6,
        out_specs=[vmem] * 5,
        scratch_shapes=[
            pltpu.VMEM((ndev, part, cols), LOW),
            pltpu.VMEM((ndev, part, cols), LOW),
            pltpu.VMEM((rows, cols), f32),
            pltpu.VMEM((rows, 2 * cols), LOW),
            pltpu.VMEM((2 * per, block, block), LOW),
            pltpu.VMEM((rows, cols), LOW),
            pltpu.VMEM((rows, cols), LOW),
            pltpu.VMEM((rows, cols), f32),
            pltpu.VMEM((ndev, part, cols), LOW),
            pltpu.VMEM((ndev, part, cols), LOW),
            dma((ndev,)),
            dma((ndev,)),
            dma((ndev,)),
            dma((ndev,)),
            dma((2,)),
            dma((2,)),
            dma((nblk,)),
            dma((nblk,)),
            dma((2,)),
        ],
        compiler_params=pltpu.CompilerParams(
            collective_id=0, has_side_effects=True, vmem_limit_bytes=48 * 1024 * 1024
        ),
    )(*inputs)
    return (outs[0],) + tuple(o[None] for o in outs[1:])


def solution(mesh):
    placed = (
        P(None, "fsdp", "tensor"),
        P(None, "fsdp", "tensor"),
        P("fsdp", None, "tensor"),
        P("fsdp", None, "tensor"),
        P("fsdp", "tensor", None, None),
        P("fsdp", "tensor", None, None),
    )
    return jax.shard_map(
        functools.partial(body, mesh.shape["fsdp"]),
        mesh=mesh,
        in_specs=placed,
        out_specs=(placed[0],) + placed[2:],
        check_vma=False,
    )
```

profile of v0, /device:TPU:1, one launch (start us, length us, event | category | flops | bytes accessed | tf_op | source)
XLA Modules:
  0.0 53.2 jit_solution(16310892729408085177)
XLA Ops:
  0.6 0.0 copy-start
  0.6 0.0 copy-start.1
  0.7 1.5 %copy.11.weights = bf16[64,28,128]{2,1,0:T(8,128)(2,1)S(1)} copy(bf16[64,28,128]{2,0,1:T(8,128)(2,1)} %param.6) | data formatting | bytes 917504 | tf_op args[0]
  2.1 1.3 %copy.12.gradient = bf16[64,28,128]{2,1,0:T(8,128)(2,1)S(1)} copy(bf16[64,28,128]{2,0,1:T(8,128)(2,1)} %param.7) | data formatting | bytes 917504 | tf_op args[1]
  3.4 0.0 copy-done
  3.4 0.0 copy-done.1
  3.5 43.8 %shard_map.101 = (bf16[64,28,128]{2,1,0:T(8,128)(2,1)S(1)}, f32[1792,128]{1,0:T(8,128)S(1)}, f32[1792,128]{1,0:T(8,128)S(1)}, f32[4,256,256]{2,1,0:T(8,128)}, f32[4,256,256]{2,1,0:T(8,128)}) custom-call(bf16[64,28,128]{2,1,0:T(8,128)(2,1)S(1)} %copy.11.weights, bf16[64,28,128]{2,1,0:T(8,128)(2,1)S(1)} %copy.12.gradient, f32[1792,128]{1,0:T(8,128)S(1)} %bitcast.8, ...), custom_call_target="tpu_custom_call" | custom-call | tf_op jit(solution)/shard_map/pallas_call | solution.py:273
  47.2 0.9 %copy.13 = bf16[64,28,128]{2,0,1:T(8,128)(2,1)} copy(bf16[64,28,128]{2,1,0:T(8,128)(2,1)S(1)} %get-tuple-element.15) | data formatting | bytes 917504
  48.2 0.9 %copy.18 = f32[1,1792,128]{2,1,0:T(8,128)} copy(f32[1,1792,128]{2,1,0:T(8,128)S(1)} %bitcast.11) | data formatting | bytes 1835008
  49.1 0.0 copy-start.3
  49.1 0.9 %copy.19 = f32[1,1792,128]{2,1,0:T(8,128)} copy(f32[1,1792,128]{2,1,0:T(8,128)S(1)} %bitcast.10) | data formatting | bytes 1835008
  50.0 0.6 %copy-done.3 = f32[4,256,256]{2,1,0:T(8,128)S(1)} copy-done((f32[4,256,256]{2,1,0:T(8,128)S(1)}, f32[4,256,256]{2,1,0:T(8,128)}, u32[]{:S(2)}) %copy-start.3) | copy-done | bytes 1048600
  50.6 0.0 copy-start.2
  50.6 1.0 %copy.20 = f32[1,4,256,256]{3,2,1,0:T(8,128)} copy(f32[1,4,256,256]{3,2,1,0:T(8,128)S(1)} %bitcast.15) | data formatting | bytes 2097152
  51.6 0.6 %copy-done.2 = f32[4,256,256]{2,1,0:T(8,128)S(1)} copy-done((f32[4,256,256]{2,1,0:T(8,128)S(1)}, f32[4,256,256]{2,1,0:T(8,128)}, u32[]{:S(2)}) %copy-start.2) | copy-done | bytes 1048600
  52.2 1.0 %copy.21 = f32[1,4,256,256]{3,2,1,0:T(8,128)} copy(f32[1,4,256,256]{3,2,1,0:T(8,128)S(1)} %bitcast.14) | data formatting | bytes 2097152
Async XLA Ops:
  0.6 2.8 %copy-start = (f32[1,1792,128]{2,1,0:T(8,128)S(1)}, f32[1,1792,128]{2,1,0:T(8,128)}, u32[]{:S(2)}) copy-start(f32[1,1792,128]{2,1,0:T(8,128)} %param.8) | copy-start | bytes 2752516
  0.6 2.8 %copy-start.1 = (f32[1,1792,128]{2,1,0:T(8,128)S(1)}, f32[1,1792,128]{2,1,0:T(8,128)}, u32[]{:S(2)}) copy-start(f32[1,1792,128]{2,1,0:T(8,128)} %param.9) | copy-start | bytes 2752516
  49.1 1.6 %copy-start.3 = (f32[4,256,256]{2,1,0:T(8,128)S(1)}, f32[4,256,256]{2,1,0:T(8,128)}, u32[]{:S(2)}) copy-start(f32[4,256,256]{2,1,0:T(8,128)} %get-tuple-element.13) | copy-start | bytes 3145732
  50.6 1.6 %copy-start.2 = (f32[4,256,256]{2,1,0:T(8,128)S(1)}, f32[4,256,256]{2,1,0:T(8,128)}, u32[]{:S(2)}) copy-start(f32[4,256,256]{2,1,0:T(8,128)} %get-tuple-element.14) | copy-start | bytes 3145732
where the time goes:
time: 53.5 us; the launch traced here: 53.2 us
  Pallas kernels  43.8 us (82%)
  local copies, waits for them, and re-layouts  8.79 us (16%)
  between operations  0.68 us (1%)
    pallas_call x1, Pallas kernels, body(): pl.pallas_call(functools.partial(kernel, ndev), out_shape=(jax.ShapeDtype...  43.8 us
    unnamed x15, local copies, waits for them, and re-layouts  8.79 us

commit v1 on v0

--- a/solution.py
+++ b/solution.py
@@ -38,7 +38,7 @@
     grad_mine, grad_other, grad_wide, grad_full, bases_low, dir_mine, dir_other,
     update_wide, update_out, update_in,
     send_grad, recv_grad, send_update, recv_update,
-    send_pair, recv_pair, send_dir, recv_dir, local_sem,
+    send_pair, recv_pair, send_share, recv_share, send_dir, recv_dir, local_sem,
 ):
     me = lax.axis_index("fsdp")
     core = lax.axis_index("tensor")
@@ -145,23 +145,34 @@
         device_id_type=MESH,
     )
     share_bases.start()
+
+    def share(i):
+        source = lax.rem(me + ndev - i, ndev)
+        return pltpu.make_async_remote_copy(
+            src_ref=grad_mine.at[source],
+            dst_ref=grad_other.at[source],
+            send_sem=send_share.at[i],
+            recv_sem=recv_share.at[i],
+            device_id=(me, other),
+            device_id_type=MESH,
+        )
+
     own.wait()
-    arrived(grad_wait)
-    share_grad = pltpu.make_async_remote_copy(
-        src_ref=grad_mine,
-        dst_ref=grad_other,
-        send_sem=send_pair.at[1],
-        recv_sem=recv_pair.at[1],
-        device_id=(me, other),
-        device_id_type=MESH,
-    )
-    share_grad.start()
+    share(0).start()
+
+    def forward(i, carry):
+        grad_wait(i).wait_recv()
+        share(i).start()
+        return carry
+
+    lax.fori_loop(1, ndev, forward, 0)
 
     for s in range(ndev):
         grad_wide[s * part : (s + 1) * part, :] = grad_mine[s].astype(jnp.float32)
     grad_full[:, my_cols] = grad_wide[...].astype(LOW)
     share_bases.wait()
-    share_grad.wait()
+    share(0).wait_recv()
+    arrived(share)
     for s in range(ndev):
         grad_wide[s * part : (s + 1) * part, :] = grad_other[s].astype(jnp.float32)
     grad_full[:, other_cols] = grad_wide[...].astype(LOW)
@@ -202,16 +213,6 @@
 
     left_gram(0)
     dir_copy(nblk - 1).start()
-    for j in range(1, per - 1):
-        left_gram(j)
-
-    @pl.when(core == 0)
-    def _():
-        left_gram(per - 1)
-
-    @pl.when(core == 1)
-    def _():
-        put_gram(per - 1, product(grad_full[...], grad_full[...], TN))
 
     right_rows = bases_low.at[nblk]
     rows_mine = right_rows[my_cols, my_cols]
@@ -226,15 +227,25 @@
     for s in range(ndev):
         update_out[s] = update_wide[s * part : (s + 1) * part, :].astype(LOW)
 
-    growns = []
-    for j in range(per):
-        grown = product3(halves(new_statistics[j]), halves(eigenbases[j]), NN)
-        growns.append(grown)
-        new_bases[j] = grown / (jnp.sqrt(jnp.sum(grown * grown)) + 1e-06)
-
+    left_gram(1)
     start(update_copy)
     own = pltpu.make_async_copy(update_out.at[me], update_in.at[me], local_sem.at[1])
     own.start()
+
+    for j in range(2, per - 1):
+        left_gram(j)
+
+    @pl.when(core == 0)
+    def _():
+        left_gram(per - 1)
+
+    @pl.when(core == 1)
+    def _():
+        put_gram(per - 1, product(grad_full[...], grad_full[...], TN))
+
+    for j in range(per):
+        grown = product3(halves(new_statistics[j]), halves(eigenbases[j]), NN)
+        new_bases[j] = grown / (jnp.sqrt(jnp.sum(grown * grown)) + 1e-06)
 
     def sweep(step, carry):
         for j in range(per):
@@ -246,6 +257,8 @@
 
     lax.fori_loop(0, NS_STEPS, sweep, 0)
     sent(grad_copy)
+    share(0).wait_send()
+    sent(share)
     own.wait()
     arrived(update_wait)
 
@@ -296,14 +309,16 @@
             dma((ndev,)),
             dma((ndev,)),
             dma((ndev,)),
-            dma((2,)),
-            dma((2,)),
+            dma((1,)),
+            dma((1,)),
+            dma((ndev,)),
+            dma((ndev,)),
             dma((nblk,)),
             dma((nblk,)),
             dma((2,)),
         ],
         compiler_params=pltpu.CompilerParams(
-            collective_id=0, has_side_effects=True, vmem_limit_bytes=48 * 1024 * 1024
+            collective_id=0, has_side_effects=True, vmem_limit_bytes=24 * 1024 * 1024
         ),
     )(*inputs)
     return (outs[0],) + tuple(o[None] for o in outs[1:])

time: 53.5 us -> 52.3 us (0.978)
  Pallas kernels: 43.8 us -> 41.5 us
  local copies, waits for them, and re-layouts: 8.79 us -> 9.93 us
    pallas_call x1, Pallas kernels: 43.8 us -> 41.5 us  [body(): pl.pallas_call(functools.partial(kernel, ndev), out_shape=(jax.ShapeDtype...]
    unnamed x15, local copies, waits for them, and re-layouts: 8.79 us -> 9.93 us
where the time goes in v1:
time: 52.3 us; the launch traced here: 52.1 us
  Pallas kernels  41.5 us (79%)
  local copies, waits for them, and re-layouts  9.93 us (19%)
  between operations  0.69 us (1%)
    pallas_call x1, Pallas kernels, body(): pl.pallas_call(functools.partial(kernel, ndev), out_shape=(jax.ShapeDtype...  41.5 us
    unnamed x15, local copies, waits for them, and re-layouts  9.93 us

profile of v1, /device:TPU:1, one launch (start us, length us, event | category | flops | bytes accessed | tf_op | source)
XLA Modules:
  0.0 52.1 jit_solution(1354858432459249799)
XLA Ops:
  0.6 0.0 copy-start
  0.6 0.0 copy-start.2
  0.7 1.5 %copy.11.weights = bf16[64,28,128]{2,1,0:T(8,128)(2,1)S(1)} copy(bf16[64,28,128]{2,0,1:T(8,128)(2,1)} %param.6) | data formatting | bytes 917504 | tf_op args[0]
  2.1 1.3 %copy.12.gradient = bf16[64,28,128]{2,1,0:T(8,128)(2,1)S(1)} copy(bf16[64,28,128]{2,0,1:T(8,128)(2,1)} %param.7) | data formatting | bytes 917504 | tf_op args[1]
  3.4 0.0 copy-done
  3.5 0.0 copy-done.2
  3.5 0.0 copy-start.1
  3.5 1.2 %copy-done.1 = f32[1,4,256,256]{3,2,1,0:T(8,128)S(1)} copy-done((f32[1,4,256,256]{3,2,1,0:T(8,128)S(1)}, f32[1,4,256,256]{3,2,1,0:T(8,128)}, u32[]{:S(2)}) %copy-start.1) | copy-done | bytes 1048600
  4.7 0.0 copy-start.3
  4.7 1.2 %copy-done.3 = f32[1,1792,128]{2,1,0:T(8,128)S(1)} copy-done((f32[1,1792,128]{2,1,0:T(8,128)S(1)}, f32[1,1792,128]{2,1,0:T(8,128)}, u32[]{:S(2)}) %copy-start.3) | copy-done | bytes 917528
  5.9 41.5 %shard_map.101 = (bf16[64,28,128]{2,1,0:T(8,128)(2,1)S(1)}, f32[1792,128]{1,0:T(8,128)S(1)}, f32[1792,128]{1,0:T(8,128)S(1)}, f32[4,256,256]{2,1,0:T(8,128)S(1)}, f32[4,256,256]{2,1,0:T(8,128)S(1)}) custom-call(bf16[64,28,128]{2,1,0:T(8,128)(2,1)S(1)} %copy.11.weights, bf16[64,28,128]{2,1,0:T(8,128)(2,1)S(1)} %copy.12.gradient, f32[1792,128]{1,0:T(8,128)S(1)} %bitcast.12, ...), custom_call_target="tpu_custom_call" | custom-call | tf_op jit(solution)/shard_map/pallas_call | solution.py:286
  47.4 0.9 %copy.13 = bf16[64,28,128]{2,0,1:T(8,128)(2,1)} copy(bf16[64,28,128]{2,1,0:T(8,128)(2,1)S(1)} %get-tuple-element.15) | data formatting | bytes 917504
  48.3 0.9 %copy.18 = f32[1,1792,128]{2,1,0:T(8,128)} copy(f32[1,1792,128]{2,1,0:T(8,128)S(1)} %bitcast.15) | data formatting | bytes 1835008
  49.2 0.9 %copy.19 = f32[1,1792,128]{2,1,0:T(8,128)} copy(f32[1,1792,128]{2,1,0:T(8,128)S(1)} %bitcast.14) | data formatting | bytes 1835008
  50.2 1.0 %copy.20 = f32[1,4,256,256]{3,2,1,0:T(8,128)} copy(f32[1,4,256,256]{3,2,1,0:T(8,128)S(1)} %bitcast.11) | data formatting | bytes 2097152
  51.1 1.0 %copy.21 = f32[1,4,256,256]{3,2,1,0:T(8,128)} copy(f32[1,4,256,256]{3,2,1,0:T(8,128)S(1)} %bitcast.10) | data formatting | bytes 2097152
Async XLA Ops:
  0.6 2.8 %copy-start = (f32[1,4,256,256]{3,2,1,0:T(8,128)S(1)}, f32[1,4,256,256]{3,2,1,0:T(8,128)}, u32[]{:S(2)}) copy-start(f32[1,4,256,256]{3,2,1,0:T(8,128)} %param.10) | copy-start | bytes 3145732
  0.6 2.8 %copy-start.2 = (f32[1,1792,128]{2,1,0:T(8,128)S(1)}, f32[1,1792,128]{2,1,0:T(8,128)}, u32[]{:S(2)}) copy-start(f32[1,1792,128]{2,1,0:T(8,128)} %param.8) | copy-start | bytes 2752516
  3.5 1.2 %copy-start.1 = (f32[1,4,256,256]{3,2,1,0:T(8,128)S(1)}, f32[1,4,256,256]{3,2,1,0:T(8,128)}, u32[]{:S(2)}) copy-start(f32[1,4,256,256]{3,2,1,0:T(8,128)} %param.11) | copy-start | bytes 3145732
  4.7 1.2 %copy-start.3 = (f32[1,1792,128]{2,1,0:T(8,128)S(1)}, f32[1,1792,128]{2,1,0:T(8,128)}, u32[]{:S(2)}) copy-start(f32[1,1792,128]{2,1,0:T(8,128)} %param.9) | copy-start | bytes 2752516

commit v2 on v1

--- a/solution.py
+++ b/solution.py
@@ -33,10 +33,11 @@
 
 def kernel(
     ndev,
-    weights, gradient, moment_first, moment_second, statistics, eigenbases,
+    weights, gradient, first_hbm, second_hbm, statistics_hbm, eigenbases_hbm,
     new_weights, new_first, new_second, new_statistics, new_bases,
     grad_mine, grad_other, grad_wide, grad_full, bases_low, dir_mine, dir_other,
     update_wide, update_out, update_in,
+    moment_first, moment_second, statistics, eigenbases,
     send_grad, recv_grad, send_update, recv_update,
     send_pair, recv_pair, send_share, recv_share, send_dir, recv_dir, local_sem,
 ):
@@ -52,8 +53,19 @@
     my_cols = pl.ds(pl.multiple_of(core * cols, cols), cols)
     other_cols = pl.ds(pl.multiple_of(other * cols, cols), cols)
 
-    for j in range(per):
-        bases_low[core * per + j] = eigenbases[j].astype(LOW)
+    loads = [
+        pltpu.make_async_copy(src, dst, local_sem.at[2 + n])
+        for n, (src, dst) in enumerate(
+            (
+                (eigenbases_hbm, eigenbases),
+                (first_hbm, moment_first),
+                (second_hbm, moment_second),
+                (statistics_hbm, statistics),
+            )
+        )
+    ]
+    for load in loads:
+        load.start()
 
     barrier = pltpu.get_barrier_semaphore()
 
@@ -65,6 +77,9 @@
 
     lax.fori_loop(1, ndev, greet, 0)
     pl.semaphore_signal(barrier, inc=1, device_id=(me, other), device_id_type=MESH)
+    loads[0].wait()
+    for j in range(per):
+        bases_low[core * per + j] = eigenbases[j].astype(LOW)
     pl.semaphore_wait(barrier, ndev)
 
     def grad_copy(i):
@@ -166,6 +181,8 @@
         return carry
 
     lax.fori_loop(1, ndev, forward, 0)
+    for load in loads[1:]:
+        load.wait()
 
     for s in range(ndev):
         grad_wide[s * part : (s + 1) * part, :] = grad_mine[s].astype(jnp.float32)
@@ -283,6 +300,9 @@
     inputs = (
         weights, gradient, moment_first[0], moment_second[0], statistics[0], eigenbases[0]
     )
+    inputs = inputs[:2] + tuple(
+        pltpu.with_memory_space_constraint(x, pltpu.HBM) for x in inputs[2:]
+    )
     outs = pl.pallas_call(
         functools.partial(kernel, ndev),
         out_shape=(
@@ -292,7 +312,7 @@
             jax.ShapeDtypeStruct((per, block, block), f32),
             jax.ShapeDtypeStruct((per, block, block), f32),
         ),
-        in_specs=[vmem] * 6,
+        in_specs=[vmem] * 2 + [pl.BlockSpec(memory_space=pltpu.HBM)] * 4,
         out_specs=[vmem] * 5,
         scratch_shapes=[
             pltpu.VMEM((ndev, part, cols), LOW),
@@ -305,6 +325,10 @@
             pltpu.VMEM((rows, cols), f32),
             pltpu.VMEM((ndev, part, cols), LOW),
             pltpu.VMEM((ndev, part, cols), LOW),
+            pltpu.VMEM((rows, cols), f32),
+            pltpu.VMEM((rows, cols), f32),
+            pltpu.VMEM((per, block, block), f32),
+            pltpu.VMEM((per, block, block), f32),
             dma((ndev,)),
             dma((ndev,)),
             dma((ndev,)),
@@ -315,7 +339,7 @@
             dma((ndev,)),
             dma((nblk,)),
             dma((nblk,)),
-            dma((2,)),
+            dma((6,)),
         ],
         compiler_params=pltpu.CompilerParams(
             collective_id=0, has_side_effects=True, vmem_limit_bytes=24 * 1024 * 1024

time: 52.3 us -> 48.7 us (0.931)
  local copies, waits for them, and re-layouts: 9.93 us -> 6.42 us
    unnamed x15 -> x9, local copies, waits for them, and re-layouts: 9.93 us -> 6.42 us
where the time goes in v2:
time: 48.7 us; the launch traced here: 48.6 us
  Pallas kernels  41.5 us (85%)
  local copies, waits for them, and re-layouts  6.42 us (13%)
  between operations  0.67 us (1%)
    pallas_call x1, Pallas kernels, body(): pl.pallas_call(functools.partial(kernel, ndev), out_shape=(jax.ShapeDtype...  41.5 us
    unnamed x9, local copies, waits for them, and re-layouts  6.42 us

profile of v2, /device:TPU:1, one launch (start us, length us, event | category | flops | bytes accessed | tf_op | source)
XLA Modules:
  0.0 48.6 jit_solution(6621168017153169286)
XLA Ops:
  0.6 0.0 copy-start
  0.6 1.4 %copy.11.weights = bf16[64,28,128]{2,1,0:T(8,128)(2,1)S(1)} copy(bf16[64,28,128]{2,0,1:T(8,128)(2,1)} %param.6) | data formatting | bytes 917504 | tf_op args[0]
  2.0 0.0 copy-done
  2.0 0.3 copy.12.gradient
  2.3 41.5 %shard_map.101 = (bf16[64,28,128]{2,1,0:T(8,128)(2,1)S(1)}, f32[1792,128]{1,0:T(8,128)S(1)}, f32[1792,128]{1,0:T(8,128)S(1)}, f32[4,256,256]{2,1,0:T(8,128)S(1)}, f32[4,256,256]{2,1,0:T(8,128)S(1)}) custom-call(bf16[64,28,128]{2,1,0:T(8,128)(2,1)S(1)} %copy.11.weights, bf16[64,28,128]{2,1,0:T(8,128)(2,1)S(1)} %copy.12.gradient, f32[1792,128]{1,0:T(8,128)} %bitcast.14, ...), custom_call_target="tpu_custom_call" | custom-call | tf_op jit(solution)/shard_map/pallas_call | solution.py:306
  43.8 0.9 %copy.13 = bf16[64,28,128]{2,0,1:T(8,128)(2,1)} copy(bf16[64,28,128]{2,1,0:T(8,128)(2,1)S(1)} %get-tuple-element.15) | data formatting | bytes 917504
  44.8 0.9 %copy.18 = f32[1,1792,128]{2,1,0:T(8,128)} copy(f32[1,1792,128]{2,1,0:T(8,128)S(1)} %bitcast.11) | data formatting | bytes 1835008
  45.7 0.9 %copy.19 = f32[1,1792,128]{2,1,0:T(8,128)} copy(f32[1,1792,128]{2,1,0:T(8,128)S(1)} %bitcast.10) | data formatting | bytes 1835008
  46.6 1.0 %copy.20 = f32[1,4,256,256]{3,2,1,0:T(8,128)} copy(f32[1,4,256,256]{3,2,1,0:T(8,128)S(1)} %bitcast.9) | data formatting | bytes 2097152
  47.6 1.0 %copy.21 = f32[1,4,256,256]{3,2,1,0:T(8,128)} copy(f32[1,4,256,256]{3,2,1,0:T(8,128)S(1)} %bitcast.8) | data formatting | bytes 2097152
Async XLA Ops:
  0.6 1.4 %copy-start = (bf16[64,28,128]{2,0,1:T(8,128)(2,1)S(1)}, bf16[64,28,128]{2,0,1:T(8,128)(2,1)}, u32[]{:S(2)}) copy-start(bf16[64,28,128]{2,0,1:T(8,128)(2,1)} %param.7) | copy-start | bytes 1376260
